TPU v7x, 32 devices: a whole 2x2x4 slice. The times are simulated.
32 devices in a mesh: tile: 4 (over x, core), tm: 8 (over z, y).
Axes of the slice: x: 2, y: 2, z: 4, core: 2. Of those that a mesh axis runs over, the one named last changes fastest.
Arguments:
- ocean_heat_anomaly: bfloat16 [256, 96, 1024], P('tm', 'tile'), may hold values from -6 to 6
- observation_reliability: bfloat16 [256, 96, 1024], P('tm', 'tile'), may hold values from 0.099609375 to 1
- swath_date_number: int32 [256], replicated, may hold values from 0 to 255, as said below
- marine_cell_flag: int32 [96, 1024], P('tile'), may hold values 0 or 1
Outputs:
- trend: float32 [256, 96, 1024], P('tm', 'tile')
Inputs may be any that keep to these rules, and one draw needn't show every extreme that they name: `swath_date_number`: every day appears exactly once; every index of tm holds the same number of granules of every block of 32 consecutive days, in no particular order.
All inputs are finite; a program needn't handle non-finite values. No bound on the sum of `marine_cell_flag` on one device may be relied on, other than what follows from the above.
Results may differ from a plain program's by a relative error of at most 0.0015.
Values may be sent and summed in bfloat16 or wider, within the bound.
No kernel may reach another device: no remote copies, remote signals or barrier semaphores. Data moves between devices by JAX's collectives and lax.ppermute only.
A program may use at most 128 MiB of HBM per device.

v0:
```python
import math
import jax
import jax.numpy as jnp
from jax import lax
from jax.sharding import PartitionSpec as P

DECAY = 0.999
UNIT = 256.0
RIDGE = 0.05


def extended(array, sides, width):
    for axis, dim in sides:
        devices, length = (lax.axis_size(axis), array.shape[dim])
        up = [(i, (i + 1) % devices) for i in range(devices - 1)]
        down = [(j, i) for i, j in up]
        last = lax.slice_in_dim(array, length - width, length, axis=dim)
        leading = lax.slice_in_dim(array, 0, width, axis=dim)
        before = lax.ppermute(last, axis, up)
        after = lax.ppermute(leading, axis, down)
        array = jnp.concatenate([before, array, after], axis=dim)
    return array


def shifted(state, length):
    zeroth, first, second, level_sum, slope_sum = state
    factor = jnp.exp(length * math.log(DECAY))
    offset = length / UNIT
    return (
        factor * zeroth,
        factor * (first + offset * zeroth),
        factor * (second + 2.0 * offset * first + offset * offset * zeroth),
        factor * level_sum,
        factor * (slope_sum + offset * level_sum),
    )


def combine(earlier, later):
    moved = shifted(earlier[:5], later[5])
    joined = tuple((moved[index] + later[index] for index in range(5)))
    return joined + (earlier[5] + later[5],)


def on_device(ocean_heat_anomaly, observation_reliability, swath_date_number, marine_cell_flag):
    ntm = lax.axis_size("tm")
    me_time = lax.axis_index("tm")
    dates_for_shard = ocean_heat_anomaly.shape[0]
    share = dates_for_shard // ntm
    ocean = marine_cell_flag.astype(jnp.float32)
    all_days = swath_date_number.reshape(ntm, dates_for_shard)
    sort_keys = (
        all_days // dates_for_shard * dates_for_shard
        + jnp.arange(dates_for_shard, dtype=jnp.int32)[None]
    )
    send_order = jnp.argsort(sort_keys, axis=1)
    sorted_days = jnp.take_along_axis(all_days, send_order, axis=1)
    shard_ranking_permutation = lax.dynamic_index_in_dim(send_order, me_time, 0, keepdims=False)
    arrived = lax.dynamic_index_in_dim(
        sorted_days.reshape(ntm, ntm, share), me_time, 1, keepdims=False
    )
    positions = arrived.reshape(dates_for_shard) - me_time * dates_for_shard
    lag = jnp.arange(dates_for_shard, dtype=jnp.int32)[:, None] - positions[None, :]
    lag_days = lag.astype(jnp.float32)
    kernel_zero = jnp.where(lag >= 0, jnp.exp(lag_days * math.log(DECAY)), jnp.float32(0.0))
    kernel_one = kernel_zero * (lag_days / UNIT)
    kernel_two = kernel_one * (lag_days / UNIT)
    weight_kernel = jnp.concatenate([kernel_zero, kernel_one, kernel_two], axis=0)
    weight_high = weight_kernel.astype(jnp.bfloat16)
    weight_low = (weight_kernel - weight_high.astype(jnp.float32)).astype(jnp.bfloat16)
    value_kernel = jnp.concatenate([kernel_zero, kernel_one], axis=0)
    ranked_anomaly_field = ocean_heat_anomaly[shard_ranking_permutation]
    sorted_quality = observation_reliability[shard_ranking_permutation]
    anomaly_slice = lax.all_to_all(
        ranked_anomaly_field, "tm", split_axis=0, concat_axis=0, tiled=True
    )
    reliability_slice = lax.all_to_all(
        sorted_quality, "tm", split_axis=0, concat_axis=0, tiled=True
    )
    pointwise_multiple = reliability_slice.astype(jnp.float32) * anomaly_slice.astype(jnp.float32)
    weight_terms = jnp.einsum(
        "ks,src->krc", weight_high, reliability_slice, preferred_element_type=jnp.float32
    ) + jnp.einsum("ks,src->krc", weight_low, reliability_slice, preferred_element_type=jnp.float32)
    value_terms = jnp.einsum(
        "ks,src->krc",
        value_kernel,
        pointwise_multiple,
        precision=lax.Precision.HIGH,
        preferred_element_type=jnp.float32,
    )
    local = (
        weight_terms[:dates_for_shard],
        weight_terms[dates_for_shard : 2 * dates_for_shard],
        weight_terms[2 * dates_for_shard :],
        value_terms[:dates_for_shard],
        value_terms[dates_for_shard:],
    )
    local = tuple((part * ocean[None] for part in local))
    totals = tuple((part[dates_for_shard - 1] for part in local)) + (jnp.float32(dates_for_shard),)
    stacked = (
        lax.all_gather(totals[0][None], "tm", axis=0, tiled=True),
        lax.all_gather(totals[1][None], "tm", axis=0, tiled=True),
        lax.all_gather(totals[2][None], "tm", axis=0, tiled=True),
        lax.all_gather(totals[3][None], "tm", axis=0, tiled=True),
        lax.all_gather(totals[4][None], "tm", axis=0, tiled=True),
    )
    empty = jnp.zeros(ocean.shape, jnp.float32)

    def fold_block(index, state):
        element = tuple(
            (lax.dynamic_index_in_dim(part, index, 0, keepdims=False) for part in stacked)
        )
        merged = combine(state, element + (jnp.float32(dates_for_shard),))
        return tuple((jnp.where(index < me_time, new, old) for new, old in zip(merged, state)))

    carried = lax.fori_loop(
        0, ntm, fold_block, (empty, empty, empty, empty, empty, jnp.float32(0.0))
    )
    offsets = jnp.arange(1, dates_for_shard + 1, dtype=jnp.float32)[:, None, None]
    moved = shifted(tuple((part[None] for part in carried[:5])), offsets)
    zeroth, first, second, level_sum, slope_sum = (
        local[index] + moved[index] for index in range(5)
    )
    det = zeroth * (second + RIDGE) - first * first
    det = jnp.where(ocean[None] > 0, det, jnp.float32(1.0))
    slope = (first * level_sum - zeroth * slope_sum) / det
    stacked_fields = jnp.concatenate([slope, ocean[None]], axis=0)
    padded = extended(stacked_fields, (("tile", 1),), 1)
    padded = jnp.pad(padded, ((0, 0), (0, 0), (1, 1)))
    rowsum = padded[:, :-2] + padded[:, 1:-1] + padded[:, 2:]
    total = rowsum[:, :, :-2] + rowsum[:, :, 1:-1] + rowsum[:, :, 2:]
    count = jnp.maximum(total[dates_for_shard], 1.0)
    return total[:dates_for_shard] / count[None]


def solution(mesh):
    in_specs = (P("tm", "tile", None), P("tm", "tile", None), P(), P("tile", None))
    out_specs = P("tm", "tile", None)
    return jax.shard_map(
        on_device, mesh=mesh, in_specs=in_specs, out_specs=out_specs, check_vma=False
    )
```

profile of v0, /device:TPU:1, one launch (start us, length us, event | category | flops | bytes accessed | tf_op | source)
XLA Modules:
  0.0 320.2 jit_solution(12389917258836446696)
XLA Ops:
  0.0 0.0 copy-start
  0.0 0.9 reshape.82
  0.9 0.1 copy.40
  1.0 0.8 sort.17
  1.8 0.2 dynamic-slice_reduce_fusion
  2.0 0.0 copy-done
  2.0 0.0 copy-start.3
  2.0 1.8 gather_fusion
  3.8 6.4 %all-to-all-start = ((bf16[32,24,1024]{2,1,0:T(8,128)(2,1)}), bf16[32,24,1024]{2,1,0:T(8,128)(2,1)S(1)}, u32[]{:S(2)}, u32[]{:S(2)}) async-start(bf16[32,24,1024]{2,1,0:T(8,128)(2,1)} %gather_fusion), calls=%async_computation | async-start | bytes 3145728 | tf_op jit(solution)/shard_map/all_to_all | solution.py:76
  10.2 1.8 gather_fusion.1
  12.0 34.4 %all-to-all-done = bf16[32,24,1024]{2,1,0:T(8,128)(2,1)S(1)} async-done(((bf16[32,24,1024]{2,1,0:T(8,128)(2,1)}), bf16[32,24,1024]{2,1,0:T(8,128)(2,1)S(1)}, u32[]{:S(2)}, u32[]{:S(2)}) %all-to-all-start) | async-done | bytes 1572896 | tf_op jit(solution)/shard_map/all_to_all | solution.py:76
  46.4 4.6 %all-to-all-start.1 = ((bf16[32,24,1024]{2,1,0:T(8,128)(2,1)}), bf16[32,24,1024]{2,1,0:T(8,128)(2,1)S(1)}, u32[]{:S(2)}, u32[]{:S(2)}) async-start(bf16[32,24,1024]{2,1,0:T(8,128)(2,1)} %gather_fusion.1), calls=%async_computation.1 | async-start | bytes 3145728 | tf_op jit(solution)/shard_map/all_to_all | solution.py:73
  51.0 0.1 copy.41
  51.1 0.1 reshape.100
  51.2 1.4 gather_fusion.2
  52.6 0.1 reshape.103
  52.7 0.7 copy.44
  53.3 0.7 dynamic-slice_subtract_fusion
  54.0 0.1 copy.45
  54.1 0.1 sub.45
  54.2 0.9 convert_element_type.27
  55.1 0.7 broadcast_in_dim.25
  55.8 0.6 fusion.27
  56.4 0.7 exponential_select_fusion
  57.1 1.5 broadcast_compare_fusion
  58.6 28.7 %all-to-all-done.1 = bf16[32,24,1024]{2,1,0:T(8,128)(2,1)S(1)} async-done(((bf16[32,24,1024]{2,1,0:T(8,128)(2,1)}), bf16[32,24,1024]{2,1,0:T(8,128)(2,1)S(1)}, u32[]{:S(2)}, u32[]{:S(2)}) %all-to-all-start.1) | async-done | bytes 1572896 | tf_op jit(solution)/shard_map/all_to_all | solution.py:73
  87.4 0.6 convert_multiply_fusion
  88.0 0.1 copy-done.7
  88.1 0.0 copy-done.8
  88.1 4.4 %fusion.6 = f32[64,24,1024]{2,0,1:T(8,128)S(1)} fusion(f32[32,24,1024]{2,1,0:T(8,128)S(1)} %convert_multiply_fusion, f32[32,32]{0,1:T(8,128)S(1)} %copy-done.8, f32[32,32]{0,1:T(8,128)S(1)} %copy-done.7), kind=kOutput, calls=%fused_computation.30 | convolution fusion | flops 301991936 | bytes 9445376 | tf_op jit(solution)/shard_map/ks,src->krc/dot_general | solution.py:83
  92.6 2.5 fusion.9
  95.1 3.0 convolution_add_fusion
  98.2 4.4 %slice_multiply_fusion.4 = (f32[32,24,1024]{2,0,1:T(8,128)S(1)}, f32[32,24,1024]{2,0,1:T(8,128)S(1)}, f32[32,24,1024]{2,0,1:T(8,128)}, f32[32,24,1024]{2,0,1:T(8,128)}, f32[32,24,1024]{2,0,1:T(8,128)}) fusion(f32[96,24,1024]{2,0,1:T(8,128)S(1)} %convolution_add_fusion, f32[24,1024]{1,0:T(8,128)S(1)} %copy-done.6, f32[64,24,1024]{2,0,1:T(8,128)S(1)} %fusion.6), kind=kLoop, calls=%fused_computation.29 | loop fusion | flops 3932160 | bytes 31555584 | tf_op jit(solution)/shard_map/mul | solution.py:97
  102.6 1.8 slice.88
  104.4 28.3 %all_gather.15 = f32[8,24,1024]{2,1,0:T(8,128)} all-gather(f32[1,24,1024]{2,1,0:T(8,128)S(1)} %copy.48), channel_id=1, replica_groups=mesh['tile'=4,'tm'=8] {'tm'}, dimensions={0}, use_global_device_ids=true | all-gather | bytes 884736 | tf_op jit(solution)/shard_map/all_gather | solution.py:100
  132.7 0.1 slice.89
  132.8 28.4 %all_gather.16 = f32[8,24,1024]{2,1,0:T(8,128)} all-gather(f32[1,24,1024]{2,1,0:T(8,128)S(1)} %copy.49), channel_id=1, replica_groups=mesh['tile'=4,'tm'=8] {'tm'}, dimensions={0}, use_global_device_ids=true | all-gather | bytes 884736 | tf_op jit(solution)/shard_map/all_gather | solution.py:101
  161.2 0.1 slice.91
  161.4 28.4 %all_gather.17 = f32[8,24,1024]{2,1,0:T(8,128)} all-gather(f32[1,24,1024]{2,1,0:T(8,128)S(1)} %copy.50), channel_id=1, replica_groups=mesh['tile'=4,'tm'=8] {'tm'}, dimensions={0}, use_global_device_ids=true | all-gather | bytes 884736 | tf_op jit(solution)/shard_map/all_gather | solution.py:102
  189.8 1.2 slice.93
  191.1 28.2 %all_gather.18 = f32[8,24,1024]{2,1,0:T(8,128)} all-gather(f32[1,24,1024]{2,1,0:T(8,128)S(1)} %copy.52), channel_id=1, replica_groups=mesh['tile'=4,'tm'=8] {'tm'}, dimensions={0}, use_global_device_ids=true | all-gather | bytes 884736 | tf_op jit(solution)/shard_map/all_gather | solution.py:103
  219.3 1.2 slice.95
  220.5 28.8 %all_gather.19 = f32[8,24,1024]{2,1,0:T(8,128)} all-gather(f32[1,24,1024]{2,1,0:T(8,128)S(1)} %copy.53), channel_id=1, replica_groups=mesh['tile'=4,'tm'=8] {'tm'}, dimensions={0}, use_global_device_ids=true | all-gather | bytes 884736 | tf_op jit(solution)/shard_map/all_gather | solution.py:104
  249.4 14.9 %while.22 = (s32[]{:T(128)}, f32[24,1024]{1,0:T(8,128)S(1)}, f32[24,1024]{1,0:T(8,128)S(1)}, f32[24,1024]{1,0:T(8,128)S(1)}, f32[24,1024]{1,0:T(8,128)S(1)}, /*i...) while((s32[]{:T(128)}, f32[24,1024]{1,0:T(8,128)S(1)}, ...), condition=%wide.region_2.3_spmd.clone, body=%wide.region_1.2_spmd.clone.sunk | while | flops 688132 | bytes 1474717 | solution.py:115
  249.4 1.8 fusion.31
  251.2 1.9 fusion.31
  253.1 1.9 fusion.31
  254.9 1.9 fusion.31
  256.8 1.9 fusion.31
  258.7 1.9 fusion.31
  260.5 1.9 fusion.31
  262.4 1.9 fusion.31
  264.3 6.6 %select_divide_fusion = f32[32,24,1024]{2,0,1:T(8,128)S(1)} fusion(f32[32,24,1024]{2,0,1:T(8,128)} %copy-done.2, f32[32,24,1024]{2,0,1:T(8,128)} %get-tuple-element.329, f32[32,24,1024]{2,0,1:T(8,128)} %get-tuple-element.324, f32[32,24,1024]{2,0,1:T(8,128)} %get-tuple-element.330, f32[32,24,1024]{2,0,1:T(8,128)S(1)} %get-tuple-element.322, ...), kind=kLoop, calls=%fused_computation.32 | loop fusion | flops 21233664 | bytes 19390976 | tf_op jit(solution)/shard_map/div | solution.py:125
  270.9 32.6 %collective-permute-start = (f32[33,1,1024]{2,0,1:T(8,128)S(1)}, f32[33,1,1024]{2,0,1:T(8,128)S(1)}, u32[]{:S(2)}, u32[]{:S(2)}) collective-permute-start(f32[33,1,1024]{2,0,1:T(8,128)S(1)} %get-tuple-element.327), channel_id=1, source_target_pairs={{0,8},{8,16},{16,24},{1,9},{9,17},{17,25},{2,10},{10,18},{18,26},{... | collective-permute-start | bytes 405512 | tf_op jit(solution)/shard_map/ppermute | solution.py:19
  303.5 1.9 collective-permute-start.1
  305.4 0.3 collective-permute-done
  305.8 4.4 %collective-permute-done.1 = f32[33,1,1024]{2,0,1:T(8,128)S(1)} collective-permute-done((f32[33,1,1024]{2,0,1:T(8,128)S(1)}, f32[33,1,1024]{2,0,1:T(8,128)S(1)}, u32[]{:S(2)}, u32[]{:S(2)}) %collective-permute-start.1) | collective-permute-done | bytes 135200 | tf_op jit(solution)/shard_map/ppermute | solution.py:20
  310.2 3.3 %select_maximum_fusion = f32[33,26,1026]{2,0,1:T(8,128)S(1)} fusion(f32[33,1,1024]{2,0,1:T(8,128)S(1)} %collective-permute-done.1, f32[33,1,1024]{2,0,1:T(8,128)S(1)} %collective-permute-done, f32[1,24,1024]{2,0,1:T(1,128)S(1)} %copy-done.4, f32[32,24,1024]{2,0,1:T(8,128)S(1)} %select_divide_fusion), kind=kLoop, calls=%fused_computation.15 | loop fusion | flops 8803080 | bytes 7035600 | tf_op jit(solution)/shard_map/concatenate | solution.py:21
  313.5 0.3 slice_add_fusion
  313.8 2.1 slice_add_fusion.2
  315.9 0.1 slice_maximum_fusion
  316.0 0.0 copy-start.1
  316.1 0.7 slice_divide_fusion
  316.7 3.5 %copy.54 = f32[32,24,1024]{2,1,0:T(8,128)} copy(f32[32,24,1024]{2,0,1:T(8,128)S(1)} %slice_divide_fusion) | data formatting | bytes 6291456 | tf_op jit(solution)/shard_map/div | solution.py:132
  (37 shorter events, 0.2 us)
Async XLA Ops:
  0.0 2.0 copy-start
  2.0 8.2 %copy-start.3 = (bf16[32,24,1024]{2,1,0:T(8,128)(2,1)S(1)}, bf16[32,24,1024]{2,1,0:T(8,128)(2,1)}, u32[]{:S(2)}) copy-start(bf16[32,24,1024]{2,1,0:T(8,128)(2,1)} %param.6) | copy-start | bytes 4718596
  3.8 42.6 %all-to-all-start = ((bf16[32,24,1024]{2,1,0:T(8,128)(2,1)}), bf16[32,24,1024]{2,1,0:T(8,128)(2,1)S(1)}, u32[]{:S(2)}, u32[]{:S(2)}) async-start(bf16[32,24,1024]{2,1,0:T(8,128)(2,1)} %gather_fusion), calls=%async_computation | async-start | bytes 3145728 | tf_op jit(solution)/shard_map/all_to_all | solution.py:76
  46.4 41.0 %all-to-all-start.1 = ((bf16[32,24,1024]{2,1,0:T(8,128)(2,1)}), bf16[32,24,1024]{2,1,0:T(8,128)(2,1)S(1)}, u32[]{:S(2)}, u32[]{:S(2)}) async-start(bf16[32,24,1024]{2,1,0:T(8,128)(2,1)} %gather_fusion.1), calls=%async_computation.1 | async-start | bytes 3145728 | tf_op jit(solution)/shard_map/all_to_all | solution.py:73
  55.1 2.0 copy-start.5
  87.4 0.7 copy-start.7
  87.4 0.7 copy-start.8
  88.1 4.4 %copy-start.9 = (f32[32,32]{0,1:T(8,128)S(1)}, f32[32,32]{0,1:T(8,128)}, u32[]{:S(2)}) copy-start(f32[32,32]{0,1:T(8,128)} %get-tuple-element.333) | copy-start | bytes 12292
  95.1 3.1 copy-start.6
  102.6 58.7 %copy-start.2 = (f32[32,24,1024]{2,0,1:T(8,128)}, f32[32,24,1024]{2,0,1:T(8,128)S(1)}, u32[]{:S(2)}) copy-start(f32[32,24,1024]{2,0,1:T(8,128)S(1)} %get-tuple-element.323) | copy-start | bytes 9437188
  249.4 14.9 %copy-start.10 = (f32[32]{0:T(128)S(1)}, f32[32]{0:T(128)}, u32[]{:S(2)}) copy-start(f32[32]{0:T(128)} %get-tuple-element.336) | copy-start | bytes 388
  249.4 14.9 %copy-start.11 = (f32[32]{0:T(128)S(1)}, f32[32]{0:T(128)}, u32[]{:S(2)}) copy-start(f32[32]{0:T(128)} %get-tuple-element.337) | copy-start | bytes 388
  264.3 6.6 %copy-start.4 = (f32[1,24,1024]{2,0,1:T(1,128)S(1)}, f32[1,24,1024]{2,0,1:T(1,128)}, u32[]{:S(2)}) copy-start(f32[1,24,1024]{2,0,1:T(1,128)} %broadcast_in_dim.25) | copy-start | bytes 294916
  270.9 34.9 %collective-permute-start = (f32[33,1,1024]{2,0,1:T(8,128)S(1)}, f32[33,1,1024]{2,0,1:T(8,128)S(1)}, u32[]{:S(2)}, u32[]{:S(2)}) collective-permute-start(f32[33,1,1024]{2,0,1:T(8,128)S(1)} %get-tuple-element.327), channel_id=1, source_target_pairs={{0,8},{8,16},{16,24},{1,9},{9,17},{17,25},{2,10},{10,18},{18,26},{... | collective-permute-start | bytes 405512 | tf_op jit(solution)/shard_map/ppermute | solution.py:19
  303.5 6.6 %collective-permute-start.1 = (f32[33,1,1024]{2,0,1:T(8,128)S(1)}, f32[33,1,1024]{2,0,1:T(8,128)S(1)}, u32[]{:S(2)}, u32[]{:S(2)}) collective-permute-start(f32[33,1,1024]{2,0,1:T(8,128)S(1)} %get-tuple-element.328), channel_id=1, source_target_pairs={{8,0},{16,8},{24,16},{9,1},{17,9},{25,17},{10,2},{18,10},{26,18},{... | collective-permute-start | bytes 405512 | tf_op jit(solution)/shard_map/ppermute | solution.py:20
  316.0 4.2 %copy-start.1 = (bf16[32,24,1024]{2,1,0:T(8,128)(2,1)S(1)}, bf16[32,24,1024]{2,1,0:T(8,128)(2,1)}, u32[]{:S(2)}) copy-start(bf16[32,24,1024]{2,1,0:T(8,128)(2,1)} %param.7) | copy-start | bytes 4718596
where the time goes:
time: 321 us; the launch traced here: 320 us
  blocking collectives  142 us (44%)
  waiting for transfers between devices  67.8 us (21%)
  starting transfers between devices  45.5 us (14%)
  other arithmetic  38.3 us (12%)
  local copies, waits for them, and re-layouts  16.1 us (5%)
  matrix products  10 us (3%)
    all_to_all x1, waiting for transfers between devices, on_device(): lax.all_to_all(sorted_quality, 'tm', split_axis=0, concat_axis=0, tiled=T...  34.4 us
    ppermute x1, starting transfers between devices, extended(): before = lax.ppermute(last, axis, up)  32.6 us
    all_gather x1, blocking collectives, on_device(): lax.all_gather(totals[4][None], 'tm', axis=0, tiled=True)  28.8 us
    all_to_all x1, waiting for transfers between devices, on_device(): lax.all_to_all(ranked_anomaly_field, 'tm', split_axis=0, concat_axis=0, t...  28.7 us
    all_gather x1, blocking collectives, on_device(): lax.all_gather(totals[2][None], 'tm', axis=0, tiled=True)  28.4 us
    all_gather x1, blocking collectives, on_device(): lax.all_gather(totals[1][None], 'tm', axis=0, tiled=True)  28.4 us
    all_gather x1, blocking collectives, on_device(): lax.all_gather(totals[0][None], 'tm', axis=0, tiled=True)  28.3 us
    all_gather x1, blocking collectives, on_device(): lax.all_gather(totals[3][None], 'tm', axis=0, tiled=True)  28.2 us
  transfers between devices with their start and end apart: 4, of which 4 were waited for; matrix products, arithmetic and copies ran while one was open for 3% of the time, Pallas kernels for 0%

commit v1 on v0

--- a/solution.py
+++ b/solution.py
@@ -7,6 +7,29 @@
 DECAY = 0.999
 UNIT = 256.0
 RIDGE = 0.05
+
+
+def cut_along(array, dim, count):
+    shape = array.shape
+    blocks = array.reshape(*shape[:dim], count, shape[dim] // count, *shape[dim + 1 :])
+    return jnp.moveaxis(blocks, dim, 0)
+
+
+def joined_along(blocks, dim):
+    shape = list(blocks.shape[1:])
+    shape[dim] *= blocks.shape[0]
+    return jnp.moveaxis(blocks, 0, dim).reshape(shape)
+
+
+def exchange_directly(value, axis, split_dim, concat_dim):
+    devices, position = (lax.axis_size(axis), lax.axis_index(axis))
+    blocks = cut_along(value, split_dim, devices)
+    outs = [blocks[position]]
+    for step in range(1, devices):
+        sent = blocks[(position + step) % devices]
+        outs.append(lax.ppermute(sent, axis, [(i, (i + step) % devices) for i in range(devices)]))
+    blocks = jnp.stack(outs)[(position - jnp.arange(devices)) % devices]
+    return joined_along(blocks, concat_dim)
 
 
 def extended(array, sides, width):
@@ -70,9 +93,7 @@
     value_kernel = jnp.concatenate([kernel_zero, kernel_one], axis=0)
     ranked_anomaly_field = ocean_heat_anomaly[shard_ranking_permutation]
     sorted_quality = observation_reliability[shard_ranking_permutation]
-    anomaly_slice = lax.all_to_all(
-        ranked_anomaly_field, "tm", split_axis=0, concat_axis=0, tiled=True
-    )
+    anomaly_slice = exchange_directly(ranked_anomaly_field, "tm", 0, 0)
     reliability_slice = lax.all_to_all(
         sorted_quality, "tm", split_axis=0, concat_axis=0, tiled=True
     )

time: 321 us -> 310 us (0.966)
  waiting for transfers between devices: 67.8 us -> 37.6 us
  local copies, waits for them, and re-layouts: 16.1 us -> 23.1 us
  blocking collectives: 142 us -> 149 us
  starting transfers between devices: 45.5 us -> 51.2 us
    all_to_all x1 -> x0, waiting for transfers between devices: 28.7 us -> none  [on_device(): lax.all_to_all(ranked_anomaly_field, 'tm', split_axis=0, concat_axis=0, t...]
    all_to_all x1, waiting for transfers between devices: 34.4 us -> 9.49 us  [on_device(): lax.all_to_all(sorted_quality, 'tm', split_axis=0, concat_axis=0, tiled=T...]
    ppermute x0 -> x7, waiting for transfers between devices: none -> 23.4 us  [exchange_directly(): lax.ppermute(sent, axis, [(i, (i + step) % devices) for i in range(device...]
    ppermute x0 -> x7, starting transfers between devices: none -> 13.3 us  [exchange_directly(): lax.ppermute(sent, axis, [(i, (i + step) % devices) for i in range(device...]
    all_gather x1, blocking collectives: 28.3 us -> 35.3 us  [on_device(): lax.all_gather(totals[0][None], 'tm', axis=0, tiled=True)]
    all_to_all x1 -> x0, starting transfers between devices: 4.63 us -> none  [on_device(): lax.all_to_all(ranked_anomaly_field, 'tm', split_axis=0, concat_axis=0, t...]
    unnamed x25 -> x39, local copies, waits for them, and re-layouts: 0.16 us -> 4.25 us
  transfers between devices with their start and end apart: 4 -> 10, of which waited for: 4 -> 6; matrix products, arithmetic and copies ran while one was open for 3% -> 5% of each run, Pallas kernels for 0% -> 0%
where the time goes in v1:
time: 310 us; the launch traced here: 309 us
  blocking collectives  149 us (48%)
  starting transfers between devices  51.2 us (17%)
  other arithmetic  37.8 us (12%)
  waiting for transfers between devices  37.6 us (12%)
  local copies, waits for them, and re-layouts  23.1 us (7%)
  matrix products  10 us (3%)
    all_gather x1, blocking collectives, on_device(): lax.all_gather(totals[0][None], 'tm', axis=0, tiled=True)  35.3 us
    ppermute x1, starting transfers between devices, extended(): before = lax.ppermute(last, axis, up)  32.2 us
    all_gather x1, blocking collectives, on_device(): lax.all_gather(totals[1][None], 'tm', axis=0, tiled=True)  29.1 us
    all_gather x1, blocking collectives, on_device(): lax.all_gather(totals[4][None], 'tm', axis=0, tiled=True)  28.9 us
    all_gather x1, blocking collectives, on_device(): lax.all_gather(totals[3][None], 'tm', axis=0, tiled=True)  28.3 us
    all_gather x1, blocking collectives, on_device(): lax.all_gather(totals[2][None], 'tm', axis=0, tiled=True)  27.6 us
    ppermute x7, waiting for transfers between devices, exchange_directly(): lax.ppermute(sent, axis, [(i, (i + step) % devices) for i in range(device...  23.4 us
    select_n x8, other arithmetic, fold_block(): jnp.where(index < me_time, new, old)  14.9 us
  transfers between devices with their start and end apart: 10, of which 6 were waited for; matrix products, arithmetic and copies ran while one was open for 5% of the time, Pallas kernels for 0%

profile of v1, /device:TPU:1, one launch (start us, length us, event | category | flops | bytes accessed | tf_op | source)
XLA Modules:
  0.0 309.3 jit_solution(8875820914899089901)
XLA Ops:
  0.0 0.9 reshape.137
  1.0 0.8 sort.17
  2.0 0.6 gather_fusion.1
  2.7 1.2 dynamic-slice_bitcast_fusion
  3.9 2.1 collective-permute-start
  6.0 1.3 collective-permute-start.1
  7.3 2.3 collective-permute-start.2
  9.5 1.0 collective-permute-start.3
  10.5 2.4 collective-permute-start.4
  12.8 1.8 gather_fusion
  14.6 3.7 %all-to-all-start = ((bf16[32,24,1024]{2,1,0:T(8,128)(2,1)}), bf16[32,24,1024]{2,1,0:T(8,128)(2,1)S(1)}, u32[]{:S(2)}, u32[]{:S(2)}) async-start(bf16[32,24,1024]{2,1,0:T(8,128)(2,1)} %gather_fusion), calls=%async_computation | async-start | bytes 3145728 | tf_op jit(solution)/shard_map/all_to_all | solution.py:97
  18.5 1.4 gather_fusion.3
  20.2 0.7 sub.58
  20.9 0.7 broadcast_in_dim.25
  21.6 0.5 multiply_exponential_fusion
  22.2 0.6 fusion.30
  22.8 0.6 pad_clamp_fusion
  23.4 0.6 broadcast_compare_fusion
  24.0 1.4 exponential_select_fusion
  25.4 3.2 %collective-permute-start.5 = (bf16[4,24,1024]{2,1,0:T(8,128)(2,1)S(1)}, bf16[4,24,1024]{2,1,0:T(8,128)(2,1)S(1)}, u32[]{:S(2)}, u32[]{:S(2)}) collective-permute-start(bf16[4,24,1024]{2,1,0:T(8,128)(2,1)S(1)} %copy-done.10), channel_id=1, source_target_pairs={{0,6},{1,7},{2,0},{3,1},{4,2},{5,3},{6,4},{7,5},{8,14},{9,15},{10,... | collective-permute-start | bytes 589832 | tf_op jit(solution)/shard_map/ppermute | solution.py:30
  28.6 0.7 bitcast_dynamic-update-slice_fusion.6
  29.3 1.2 collective-permute-start.6
  30.5 0.7 bitcast_dynamic-update-slice_fusion.5
  31.1 1.1 collective-permute-done.2
  32.2 0.7 bitcast_dynamic-update-slice_fusion.4
  32.9 0.7 bitcast_dynamic-update-slice_fusion.3
  33.6 0.7 bitcast_dynamic-update-slice_fusion.2
  34.3 18.8 %collective-permute-done.5 = bf16[4,24,1024]{2,1,0:T(8,128)(2,1)S(1)} collective-permute-done((bf16[4,24,1024]{2,1,0:T(8,128)(2,1)S(1)}, bf16[4,24,1024]{2,1,0:T(8,128)(2,1)S(1)}, u32[]{:S(2)}, u32[]{:S(2)}) %collective-permute-start.5) | collective-permute-done | bytes 196640 | tf_op jit(solution)/shard_map/ppermute | solution.py:30
  53.1 0.7 bitcast_dynamic-update-slice_fusion.1
  53.8 3.5 %collective-permute-done.6 = bf16[4,24,1024]{2,1,0:T(8,128)(2,1)S(1)} collective-permute-done((bf16[4,24,1024]{2,1,0:T(8,128)(2,1)S(1)}, bf16[4,24,1024]{2,1,0:T(8,128)(2,1)S(1)}, u32[]{:S(2)}, u32[]{:S(2)}) %collective-permute-start.6) | collective-permute-done | bytes 196640 | tf_op jit(solution)/shard_map/ppermute | solution.py:30
  57.3 0.7 bitcast_dynamic-update-slice_fusion
  58.0 2.2 gather_fusion.2
  60.2 9.5 %all-to-all-done = bf16[32,24,1024]{2,1,0:T(8,128)(2,1)S(1)} async-done(((bf16[32,24,1024]{2,1,0:T(8,128)(2,1)}), bf16[32,24,1024]{2,1,0:T(8,128)(2,1)S(1)}, u32[]{:S(2)}, u32[]{:S(2)}) %all-to-all-start) | async-done | bytes 1572896 | tf_op jit(solution)/shard_map/all_to_all | solution.py:97
  69.7 0.7 convert_multiply_fusion
  70.4 4.4 %fusion.6 = f32[64,24,1024]{2,0,1:T(8,128)S(1)} fusion(f32[32,24,1024]{2,1,0:T(8,128)S(1)} %convert_multiply_fusion, f32[32,32]{0,1:T(8,128)S(1)} %copy-done.8, f32[32,32]{0,1:T(8,128)S(1)} %get-tuple-element.339), kind=kOutput, calls=%fused_computation.32 | convolution fusion | flops 301991936 | bytes 9445376 | tf_op jit(solution)/shard_map/ks,src->krc/dot_general | solution.py:104
  74.9 2.5 fusion.9
  77.4 3.1 convolution_add_fusion
  80.5 4.4 %slice_multiply_fusion.4 = (f32[32,24,1024]{2,0,1:T(8,128)S(1)}, f32[32,24,1024]{2,0,1:T(8,128)S(1)}, f32[32,24,1024]{2,0,1:T(8,128)}, f32[32,24,1024]{2,0,1:T(8,128)}, f32[32,24,1024]{2,0,1:T(8,128)}) fusion(f32[96,24,1024]{2,0,1:T(8,128)S(1)} %convolution_add_fusion, f32[24,1024]{1,0:T(8,128)S(1)} %copy-done.6, f32[64,24,1024]{2,0,1:T(8,128)S(1)} %fusion.6), kind=kLoop, calls=%fused_computation.30 | loop fusion | flops 3932160 | bytes 31555584 | tf_op jit(solution)/shard_map/mul | solution.py:118
  84.9 1.8 slice.90
  86.8 35.3 %all_gather.15 = f32[8,24,1024]{2,1,0:T(8,128)} all-gather(f32[1,24,1024]{2,1,0:T(8,128)S(1)} %copy.48), channel_id=1, replica_groups=mesh['tile'=4,'tm'=8] {'tm'}, dimensions={0}, use_global_device_ids=true | all-gather | bytes 884736 | tf_op jit(solution)/shard_map/all_gather | solution.py:121
  122.1 29.1 %all_gather.16 = f32[8,24,1024]{2,1,0:T(8,128)} all-gather(f32[1,24,1024]{2,1,0:T(8,128)S(1)} %copy.49), channel_id=1, replica_groups=mesh['tile'=4,'tm'=8] {'tm'}, dimensions={0}, use_global_device_ids=true | all-gather | bytes 884736 | tf_op jit(solution)/shard_map/all_gather | solution.py:122
  151.4 27.6 %all_gather.17 = f32[8,24,1024]{2,1,0:T(8,128)} all-gather(f32[1,24,1024]{2,1,0:T(8,128)S(1)} %copy.50), channel_id=1, replica_groups=mesh['tile'=4,'tm'=8] {'tm'}, dimensions={0}, use_global_device_ids=true | all-gather | bytes 884736 | tf_op jit(solution)/shard_map/all_gather | solution.py:123
  179.0 1.2 slice.95
  180.2 28.3 %all_gather.18 = f32[8,24,1024]{2,1,0:T(8,128)} all-gather(f32[1,24,1024]{2,1,0:T(8,128)S(1)} %copy.52), channel_id=1, replica_groups=mesh['tile'=4,'tm'=8] {'tm'}, dimensions={0}, use_global_device_ids=true | all-gather | bytes 884736 | tf_op jit(solution)/shard_map/all_gather | solution.py:124
  208.5 1.2 slice.97
  209.8 28.9 %all_gather.19 = f32[8,24,1024]{2,1,0:T(8,128)} all-gather(f32[1,24,1024]{2,1,0:T(8,128)S(1)} %copy.53), channel_id=1, replica_groups=mesh['tile'=4,'tm'=8] {'tm'}, dimensions={0}, use_global_device_ids=true | all-gather | bytes 884736 | tf_op jit(solution)/shard_map/all_gather | solution.py:125
  238.7 15.0 %while.22 = (s32[]{:T(128)}, f32[24,1024]{1,0:T(8,128)S(1)}, f32[24,1024]{1,0:T(8,128)S(1)}, f32[24,1024]{1,0:T(8,128)S(1)}, f32[24,1024]{1,0:T(8,128)S(1)}, /*i...) while((s32[]{:T(128)}, f32[24,1024]{1,0:T(8,128)S(1)}, ...), condition=%wide.region_2.3_spmd.clone, body=%wide.region_1.2_spmd.clone.sunk | while | flops 688132 | bytes 1474717 | solution.py:136
  238.7 1.8 fusion.34
  240.6 1.9 fusion.34
  242.4 1.9 fusion.34
  244.3 1.9 fusion.34
  246.2 1.9 fusion.34
  248.1 1.9 fusion.34
  249.9 1.9 fusion.34
  251.8 1.9 fusion.34
  253.7 6.6 %select_divide_fusion = f32[32,24,1024]{2,0,1:T(8,128)S(1)} fusion(f32[32,24,1024]{2,0,1:T(8,128)} %copy-done.2, f32[32,24,1024]{2,0,1:T(8,128)} %get-tuple-element.337, f32[32,24,1024]{2,0,1:T(8,128)} %get-tuple-element.324, f32[32,24,1024]{2,0,1:T(8,128)} %get-tuple-element.338, f32[32,24,1024]{2,0,1:T(8,128)S(1)} %get-tuple-element.322, ...), kind=kLoop, calls=%fused_computation.34 | loop fusion | flops 21233664 | bytes 19390976 | tf_op jit(solution)/shard_map/div | solution.py:146
  260.3 32.2 %collective-permute-start.7 = (f32[33,1,1024]{2,0,1:T(8,128)S(1)}, f32[33,1,1024]{2,0,1:T(8,128)S(1)}, u32[]{:S(2)}, u32[]{:S(2)}) collective-permute-start(f32[33,1,1024]{2,0,1:T(8,128)S(1)} %get-tuple-element.327), channel_id=1, source_target_pairs={{0,8},{8,16},{16,24},{1,9},{9,17},{17,25},{2,10},{10,18},{18,26},{... | collective-permute-start | bytes 405512 | tf_op jit(solution)/shard_map/ppermute | solution.py:42
  292.6 1.9 collective-permute-start.8
  294.8 4.4 %collective-permute-done.8 = f32[33,1,1024]{2,0,1:T(8,128)S(1)} collective-permute-done((f32[33,1,1024]{2,0,1:T(8,128)S(1)}, f32[33,1,1024]{2,0,1:T(8,128)S(1)}, u32[]{:S(2)}, u32[]{:S(2)}) %collective-permute-start.8) | collective-permute-done | bytes 135200 | tf_op jit(solution)/shard_map/ppermute | solution.py:43
  299.2 3.3 %select_maximum_fusion = f32[33,26,1026]{2,0,1:T(8,128)S(1)} fusion(f32[33,1,1024]{2,0,1:T(8,128)S(1)} %collective-permute-done.8, f32[33,1,1024]{2,0,1:T(8,128)S(1)} %collective-permute-done.7, f32[1,24,1024]{2,0,1:T(1,128)S(1)} %copy-done.4, f32[32,24,1024]{2,0,1:T(8,128)S(1)} %select_divide_fusion), kind=kLoop, calls=%fused_computation.16 | loop fusion | flops 8803080 | bytes 7035600 | tf_op jit(solution)/shard_map/concatenate | solution.py:44
  302.6 0.3 slice_add_fusion
  302.9 2.1 slice_add_fusion.2
  305.1 0.7 slice_divide_fusion
  305.8 3.5 %copy.54 = f32[32,24,1024]{2,1,0:T(8,128)} copy(f32[32,24,1024]{2,0,1:T(8,128)S(1)} %slice_divide_fusion) | data formatting | bytes 6291456 | tf_op jit(solution)/shard_map/div | solution.py:153
  (68 shorter events, 1.5 us)
Async XLA Ops:
  0.0 2.0 copy-start
  2.7 10.1 %copy-start.3 = (bf16[32,24,1024]{2,1,0:T(8,128)(2,1)S(1)}, bf16[32,24,1024]{2,1,0:T(8,128)(2,1)}, u32[]{:S(2)}) copy-start(bf16[32,24,1024]{2,1,0:T(8,128)(2,1)} %param.7) | copy-start | bytes 4718596
  3.9 21.5 %collective-permute-start = (bf16[4,24,1024]{2,1,0:T(8,128)(2,1)}, bf16[4,24,1024]{2,1,0:T(8,128)(2,1)S(1)}, u32[]{:S(2)}, u32[]{:S(2)}) collective-permute-start(bf16[4,24,1024]{2,1,0:T(8,128)(2,1)} %get-tuple-element.335), channel_id=1, source_target_pairs={{0,1},{1,2},{2,3},{3,4},{4,5},{5,6},{6,7},{7,0},{8,9},{9,10},{10,1... | collective-permute-start | bytes 589832 | tf_op jit(solution)/shard_map/ppermute | solution.py:30
  6.0 23.3 %collective-permute-start.1 = (bf16[4,24,1024]{2,1,0:T(8,128)(2,1)}, bf16[4,24,1024]{2,1,0:T(8,128)(2,1)S(1)}, u32[]{:S(2)}, u32[]{:S(2)}) collective-permute-start(bf16[4,24,1024]{2,1,0:T(8,128)(2,1)} %get-tuple-element.334), channel_id=1, source_target_pairs={{0,2},{1,3},{2,4},{3,5},{4,6},{5,7},{6,0},{7,1},{8,10},{9,11},{10,... | collective-permute-start | bytes 589832 | tf_op jit(solution)/shard_map/ppermute | solution.py:30
  7.3 25.0 %collective-permute-start.2 = (bf16[4,24,1024]{2,1,0:T(8,128)(2,1)}, bf16[4,24,1024]{2,1,0:T(8,128)(2,1)S(1)}, u32[]{:S(2)}, u32[]{:S(2)}) collective-permute-start(bf16[4,24,1024]{2,1,0:T(8,128)(2,1)} %get-tuple-element.333), channel_id=1, source_target_pairs={{0,3},{1,4},{2,5},{3,6},{4,7},{5,0},{6,1},{7,2},{8,11},{9,12},{10,... | collective-permute-start | bytes 589832 | tf_op jit(solution)/shard_map/ppermute | solution.py:30
  9.5 23.4 %collective-permute-start.3 = (bf16[4,24,1024]{2,1,0:T(8,128)(2,1)}, bf16[4,24,1024]{2,1,0:T(8,128)(2,1)S(1)}, u32[]{:S(2)}, u32[]{:S(2)}) collective-permute-start(bf16[4,24,1024]{2,1,0:T(8,128)(2,1)} %get-tuple-element.332), channel_id=1, source_target_pairs={{0,4},{1,5},{2,6},{3,7},{4,0},{5,1},{6,2},{7,3},{8,12},{9,13},{10,... | collective-permute-start | bytes 589832 | tf_op jit(solution)/shard_map/ppermute | solution.py:30
  10.5 23.1 %collective-permute-start.4 = (bf16[4,24,1024]{2,1,0:T(8,128)(2,1)}, bf16[4,24,1024]{2,1,0:T(8,128)(2,1)S(1)}, u32[]{:S(2)}, u32[]{:S(2)}) collective-permute-start(bf16[4,24,1024]{2,1,0:T(8,128)(2,1)} %get-tuple-element.331), channel_id=1, source_target_pairs={{0,5},{1,6},{2,7},{3,0},{4,1},{5,2},{6,3},{7,4},{8,13},{9,14},{10,... | collective-permute-start | bytes 589832 | tf_op jit(solution)/shard_map/ppermute | solution.py:30
  14.6 6.3 %copy-start.7 = (s32[24,1024]{1,0:T(8,128)S(1)}, s32[24,1024]{1,0:T(8,128)}, u32[]{:S(2)}) copy-start(s32[24,1024]{1,0:T(8,128)} %param.9) | copy-start | bytes 294916
  14.6 55.0 %all-to-all-start = ((bf16[32,24,1024]{2,1,0:T(8,128)(2,1)}), bf16[32,24,1024]{2,1,0:T(8,128)(2,1)S(1)}, u32[]{:S(2)}, u32[]{:S(2)}) async-start(bf16[32,24,1024]{2,1,0:T(8,128)(2,1)} %gather_fusion), calls=%async_computation | async-start | bytes 3145728 | tf_op jit(solution)/shard_map/all_to_all | solution.py:97
  18.3 7.0 %copy-start.10 = (bf16[4,24,1024]{2,1,0:T(8,128)(2,1)S(1)}, bf16[4,24,1024]{2,1,0:T(8,128)(2,1)}, u32[]{:S(2)}) copy-start(bf16[4,24,1024]{2,1,0:T(8,128)(2,1)} %get-tuple-element.330) | copy-start | bytes 589828
  18.4 10.9 %copy-start.9 = (bf16[4,24,1024]{2,1,0:T(8,128)(2,1)S(1)}, bf16[4,24,1024]{2,1,0:T(8,128)(2,1)}, u32[]{:S(2)}) copy-start(bf16[4,24,1024]{2,1,0:T(8,128)(2,1)} %get-tuple-element.329) | copy-start | bytes 589828
  20.9 36.4 %copy-start.5 = (f32[24,1024]{1,0:T(8,128)}, f32[24,1024]{1,0:T(8,128)S(1)}, u32[]{:S(2)}) copy-start(f32[24,1024]{1,0:T(8,128)S(1)} %convert_element_type.30) | copy-start | bytes 294916
  25.4 27.7 %collective-permute-start.5 = (bf16[4,24,1024]{2,1,0:T(8,128)(2,1)S(1)}, bf16[4,24,1024]{2,1,0:T(8,128)(2,1)S(1)}, u32[]{:S(2)}, u32[]{:S(2)}) collective-permute-start(bf16[4,24,1024]{2,1,0:T(8,128)(2,1)S(1)} %copy-done.10), channel_id=1, source_target_pairs={{0,6},{1,7},{2,0},{3,1},{4,2},{5,3},{6,4},{7,5},{8,14},{9,15},{10,... | collective-permute-start | bytes 589832 | tf_op jit(solution)/shard_map/ppermute | solution.py:30
  29.3 28.0 %collective-permute-start.6 = (bf16[4,24,1024]{2,1,0:T(8,128)(2,1)S(1)}, bf16[4,24,1024]{2,1,0:T(8,128)(2,1)S(1)}, u32[]{:S(2)}, u32[]{:S(2)}) collective-permute-start(bf16[4,24,1024]{2,1,0:T(8,128)(2,1)S(1)} %copy-done.9), channel_id=1, source_target_pairs={{0,7},{1,0},{2,1},{3,2},{4,3},{5,4},{6,5},{7,6},{8,15},{9,8},{10,9... | collective-permute-start | bytes 589832 | tf_op jit(solution)/shard_map/ppermute | solution.py:30
  69.7 0.7 copy-start.8
  70.4 4.5 %copy-start.11 = (f32[32,32]{0,1:T(8,128)S(1)}, f32[32,32]{0,1:T(8,128)}, u32[]{:S(2)}) copy-start(f32[32,32]{0,1:T(8,128)} %get-tuple-element.341) | copy-start | bytes 12292
  77.4 3.1 copy-start.6
  84.9 66.3 %copy-start.2 = (f32[32,24,1024]{2,0,1:T(8,128)}, f32[32,24,1024]{2,0,1:T(8,128)S(1)}, u32[]{:S(2)}) copy-start(f32[32,24,1024]{2,0,1:T(8,128)S(1)} %get-tuple-element.323) | copy-start | bytes 9437188
  238.7 15.0 %copy-start.12 = (f32[32]{0:T(128)S(1)}, f32[32]{0:T(128)}, u32[]{:S(2)}) copy-start(f32[32]{0:T(128)} %get-tuple-element.342) | copy-start | bytes 388
  238.7 15.0 %copy-start.13 = (f32[32]{0:T(128)S(1)}, f32[32]{0:T(128)}, u32[]{:S(2)}) copy-start(f32[32]{0:T(128)} %get-tuple-element.343) | copy-start | bytes 388
  238.7 15.0 %copy-start.14 = (f32[32]{0:T(128)S(1)}, f32[32]{0:T(128)}, u32[]{:S(2)}) copy-start(f32[32]{0:T(128)} %get-tuple-element.344) | copy-start | bytes 388
  238.7 15.0 %copy-start.15 = (f32[32]{0:T(128)S(1)}, f32[32]{0:T(128)}, u32[]{:S(2)}) copy-start(f32[32]{0:T(128)} %get-tuple-element.345) | copy-start | bytes 388
  253.7 6.6 %copy-start.4 = (f32[1,24,1024]{2,0,1:T(1,128)S(1)}, f32[1,24,1024]{2,0,1:T(1,128)}, u32[]{:S(2)}) copy-start(f32[1,24,1024]{2,0,1:T(1,128)} %broadcast_in_dim.25) | copy-start | bytes 294916
  260.3 34.5 %collective-permute-start.7 = (f32[33,1,1024]{2,0,1:T(8,128)S(1)}, f32[33,1,1024]{2,0,1:T(8,128)S(1)}, u32[]{:S(2)}, u32[]{:S(2)}) collective-permute-start(f32[33,1,1024]{2,0,1:T(8,128)S(1)} %get-tuple-element.327), channel_id=1, source_target_pairs={{0,8},{8,16},{16,24},{1,9},{9,17},{17,25},{2,10},{10,18},{18,26},{... | collective-permute-start | bytes 405512 | tf_op jit(solution)/shard_map/ppermute | solution.py:42
  292.6 6.6 %collective-permute-start.8 = (f32[33,1,1024]{2,0,1:T(8,128)S(1)}, f32[33,1,1024]{2,0,1:T(8,128)S(1)}, u32[]{:S(2)}, u32[]{:S(2)}) collective-permute-start(f32[33,1,1024]{2,0,1:T(8,128)S(1)} %get-tuple-element.328), channel_id=1, source_target_pairs={{8,0},{16,8},{24,16},{9,1},{17,9},{25,17},{10,2},{18,10},{26,18},{... | collective-permute-start | bytes 405512 | tf_op jit(solution)/shard_map/ppermute | solution.py:43
  305.1 4.2 %copy-start.1 = (bf16[32,24,1024]{2,1,0:T(8,128)(2,1)S(1)}, bf16[32,24,1024]{2,1,0:T(8,128)(2,1)}, u32[]{:S(2)}) copy-start(bf16[32,24,1024]{2,1,0:T(8,128)(2,1)} %param.6) | copy-start | bytes 4718596
